TPU v7x, 32 devices: a whole 2x2x4 slice. The times are simulated.
32 devices in a mesh: row: 8 (over z, x), col: 4 (over y, core).
Axes of the slice: x: 2, y: 2, z: 4, core: 2. Of those that a mesh axis runs over, the one named last changes fastest.
Arguments:
- geneo_vectors: bfloat16 [32, 32, 512, 512], P(None, None, 'row', 'col'), as said below
- phase_labels: int32 [32, 512, 512], P(None, 'row', 'col'), may hold values from 0 to 3, as said below
- phase_mobility: float32 [4], replicated, may hold values from 0.5 to 5
Outputs:
- coarse_factor: float32 [32, 4, 4, 2, 2, 8, 2, 32], P(None, None, 'col', None, None, 'row')
Inputs may be any that keep to these rules, and one draw needn't show every extreme that they name: `geneo_vectors`: the 32 vectors of each subdomain are linearly independent on its cells. `phase_labels`: within one subdomain the labels take one or two values, some q and (q + 1) modulo 4.
All inputs are finite; a program needn't handle non-finite values.
Results may differ from a plain program's by a relative error of at most 0.00055.
Values may be sent and summed in bfloat16 or wider, within the bound.
A program may use at most 512 MiB of HBM per device.

v0:
```python
import jax
import jax.numpy as jnp
from jax import lax
from jax.sharding import PartitionSpec as P

NB = 2
PSUB = 2
FACES = ((-1, 0), (1, 0), (0, -1), (0, 1))


def with_halo(cells, sides, width):
    for axis, dim in sides:
        count = lax.axis_size(axis)
        ends = count - 1
        head = lax.slice_in_dim(cells, 0, width, axis=dim)
        tail = lax.slice_in_dim(cells, cells.shape[dim] - width, cells.shape[dim], axis=dim)
        cells = jnp.concatenate(
            [
                lax.ppermute(tail, axis, [(i, (i + 1) % count) for i in range(ends)]),
                cells,
                lax.ppermute(head, axis, [((i + 1) % count, i) for i in range(ends)]),
            ],
            axis=dim,
        )
    return cells


def slot_offsets():
    offsets = [((0, 0), (0, 0))]
    for face in FACES:
        offsets += [((0, 0), face), (face, (0, 0)), (face, face)]
    for face_x in FACES[:2]:
        for face_y in FACES[2:]:
            offsets += [(face_x, face_y), (face_y, face_x)]
    return offsets


def band_index(from_off, to_off):
    return (to_off[0] - from_off[0] + 1) * 3 + (to_off[1] - from_off[1] + 1)


def from_next(field, axis):
    count = field.shape[axis]
    inner = lax.slice_in_dim(field, 1, count, axis=axis)
    blank = jnp.zeros_like(lax.slice_in_dim(field, 0, 1, axis=axis))
    return jnp.concatenate([inner, blank], axis=axis)


def from_prev(field, axis):
    count = field.shape[axis]
    inner = lax.slice_in_dim(field, 0, count - 1, axis=axis)
    blank = jnp.zeros_like(lax.slice_in_dim(field, 0, 1, axis=axis))
    return jnp.concatenate([blank, inner], axis=axis)


def laplace_own(own):
    field = own.astype(jnp.float32)
    near = from_next(field, 1) + from_prev(field, 1)
    near = near + from_next(field, 2) + from_prev(field, 2)
    near = near + from_next(field, 3) + from_prev(field, 3)
    return near - 6.0 * field


def contract_cells(left, right):
    flat_left = left.reshape(left.shape[0], -1)
    flat_right = right.reshape(right.shape[0], -1)
    return lax.dot_general(
        flat_left, flat_right, (((1,), (1,)), ((), ())), preferred_element_type=jnp.float32
    )


def local_tiles(own, labels, mobility_table):
    rims_x = jnp.stack([own[:, :, 0, :], own[:, :, -1, :]], axis=2)
    wide_x = with_halo(rims_x, (("row", 2),), 1)
    rims_y = jnp.stack([own[:, :, :, 0], own[:, :, :, -1]], axis=2)
    wide_y = with_halo(rims_y, (("col", 2),), 1)
    lower_x = wide_x[:, :, 0, :]
    upper_x = wide_x[:, :, 3, :]
    lower_y = wide_y[:, :, 0, :]
    upper_y = wide_y[:, :, 3, :]
    root_table = jnp.sqrt(mobility_table)
    cell_root = jnp.zeros(labels.shape, jnp.float32)
    for phase in range(mobility_table.shape[0]):
        cell_root = cell_root + jnp.where(labels == phase, root_table[phase], jnp.float32(0.0))
    flux = (laplace_own(own) * cell_root).astype(jnp.bfloat16)
    tiles = [contract_cells(own, own) + contract_cells(flux, flux)]
    face_data = [
        (flux[:, :, 0, :], lower_x, cell_root[:, 0, :]),
        (flux[:, :, -1, :], upper_x, cell_root[:, -1, :]),
        (flux[:, :, :, 0], lower_y, cell_root[:, :, 0]),
        (flux[:, :, :, -1], upper_y, cell_root[:, :, -1]),
    ]
    for layer_f, layer_z, layer_r in face_data:
        across = (layer_z.astype(jnp.float32) * layer_r).astype(jnp.bfloat16)
        cross = contract_cells(layer_f, across)
        tiles += [cross, cross.T, contract_cells(across, across)]
    for x_first in (True, False):
        for y_first in (True, False):
            layer_x = lower_x if x_first else upper_x
            layer_y = lower_y if y_first else upper_y
            cell_x = 0 if x_first else -1
            cell_y = 0 if y_first else -1
            corner_r = cell_root[:, cell_x, cell_y]
            along_x = (layer_x[:, :, cell_y].astype(jnp.float32) * corner_r).astype(jnp.bfloat16)
            along_y = (layer_y[:, :, cell_x].astype(jnp.float32) * corner_r).astype(jnp.bfloat16)
            pair = contract_cells(along_x, along_y)
            tiles += [pair, pair.T]
    return jnp.stack(tiles)


def shift_grid(values, offset):
    widths = [(1, 1), (1, 1)] + [(0, 0)] * (values.ndim - 2)
    padded = jnp.pad(values, widths)
    start_x = 1 - offset[0]
    start_y = 1 - offset[1]
    return padded[start_x : start_x + values.shape[0], start_y : start_y + values.shape[1]]


def to_owner(stack, n_row, n_col):
    slots = stack.shape[0]
    vectors = stack.shape[1]
    row_blocks = vectors // (NB * n_row)
    col_blocks = vectors // (NB * n_col)
    split = stack.reshape(slots, row_blocks, n_row, NB, col_blocks, n_col, NB)
    moved = split.transpose(2, 5, 0, 4, 6, 1, 3)
    return moved.reshape(n_row, n_col, slots * col_blocks * NB * row_blocks * NB)


def place_bands(bands, n_row, n_col):
    n_sub = n_row * n_col
    sub_x = jnp.arange(n_sub, dtype=jnp.int32) // n_col
    sub_y = jnp.arange(n_sub, dtype=jnp.int32) % n_col
    total = None
    for index in range(9):
        step_x = index // 3 - 1
        step_y = index % 3 - 1
        match = (
            (sub_x[:, None] == sub_x[None, :] + step_x)
            & (sub_y[:, None] == sub_y[None, :] + step_y)
        ).astype(jnp.float32)
        flat = bands[index].reshape(n_sub, -1).T
        term = match[:, None, :] * flat[None, :, :]
        total = term if total is None else total + term
    return total


def body(geneo_vectors, phase_labels, phase_mobility):
    vectors = geneo_vectors.shape[0]
    n_row = lax.axis_size("row")
    n_col = lax.axis_size("col")
    n_sub = n_row * n_col
    row_blocks = vectors // (NB * n_row)
    col_blocks = vectors // (NB * n_col)
    rows_here = row_blocks * NB * n_sub
    piece_len = col_blocks * NB * row_blocks * NB
    width = PSUB * vectors
    tiles = local_tiles(geneo_vectors, phase_labels, phase_mobility)
    offsets = slot_offsets()
    routed = lax.all_to_all(
        lax.all_to_all(
            to_owner(tiles, n_row, n_col), "row", split_axis=0, concat_axis=0, tiled=True
        ),
        "col",
        split_axis=1,
        concat_axis=1,
        tiled=True,
    )
    routed = routed.reshape(n_row, n_col, len(offsets), piece_len)
    bands = [jnp.zeros((n_row, n_col, piece_len), jnp.float32) for count in range(9)]
    for slot, pair_off in enumerate(offsets):
        place = band_index(pair_off[0], pair_off[1])
        bands[place] = bands[place] + shift_grid(routed[:, :, slot], pair_off[0])
    local = place_bands(bands, n_row, n_col).reshape(n_sub, col_blocks * NB, rows_here)
    col_index = lax.axis_index("col")
    row_sub = jnp.arange(rows_here, dtype=jnp.int32) % n_sub
    col_sub = jnp.arange(n_sub, dtype=jnp.int32)
    for panel in range(2):
        first = panel * PSUB
        last = first + PSUB
        part = local[first:last].reshape(PSUB, col_blocks, 1, NB, rows_here)
        whole = lax.all_gather(part, "col", axis=2, tiled=True).reshape(width, rows_here)
        diag_part = whole.reshape(width, row_blocks, 1, NB, n_sub)[:, :, :, :, first:last]
        diag_all = lax.all_gather(diag_part, "row", axis=2, tiled=True)
        diag = diag_all.transpose(0, 4, 1, 2, 3).reshape(width, width).T
        low = jnp.linalg.cholesky(diag)
        solved = lax.linalg.triangular_solve(low, whole, left_side=True, lower=True)
        solved = jnp.where(row_sub[None, :] >= first, solved, jnp.float32(0.0))
        mine = lax.dynamic_index_in_dim(
            solved.reshape(PSUB, col_blocks, n_col, NB, rows_here), col_index, 2, keepdims=False
        )
        local = local.at[first:last].set(mine.reshape(PSUB, col_blocks * NB, rows_here))
        gathered = lax.all_gather(
            solved.reshape(width, row_blocks, 1, NB, n_sub).astype(jnp.bfloat16),
            "row",
            axis=2,
            tiled=True,
        ).astype(jnp.float32)
        picked = lax.dynamic_index_in_dim(
            gathered.reshape(width, row_blocks, n_row // n_col, n_col, NB, n_sub),
            col_index,
            3,
            keepdims=False,
        )
        columns = (
            picked.reshape(width, col_blocks, NB, n_sub)
            .transpose(0, 3, 1, 2)
            .reshape(width, n_sub * col_blocks * NB)
        )
        update = lax.dot_general(
            columns,
            solved,
            (((0,), (0,)), ((), ())),
            precision=lax.Precision.HIGHEST,
            preferred_element_type=jnp.float32,
        )
        update = update.reshape(n_sub, col_blocks * NB, rows_here)
        trailing = (col_sub >= last)[:, None, None]
        above = (row_sub < last)[None, None, :]
        local = jnp.where(trailing, jnp.where(above, jnp.float32(0.0), local - update), local)
    return local.reshape(n_sub, col_blocks, 1, NB, row_blocks, 1, NB, n_sub)


def solution(mesh):
    return jax.shard_map(
        body,
        mesh=mesh,
        in_specs=(P(None, None, "row", "col"), P(None, "row", "col"), P()),
        out_specs=P(None, None, "col", None, None, "row", None, None),
        check_vma=False,
    )
```

profile of v0, /device:TPU:0, one launch (start us, length us, event | category | flops | bytes accessed | tf_op | source)
XLA Modules:
  0.0 737.6 jit_solution(1888599617356064845)
XLA Ops:
  0.0 25.4 %fusion.90 = (bf16[32,32,64,1]{3,2,1,0:T(8,128)(2,1)}, bf16[32,32,64,1]{3,2,1,0:T(8,128)(2,1)}) fusion(bf16[32,32,64,128]{3,2,1,0:T(8,128)(2,1)} %param.10), kind=kLoop, calls=%fused_computation.168 | loop fusion | bytes 524288 | tf_op jit(solution)/shard_map/slice | solution.py:75
  25.4 19.4 %copy.541 = bf16[32,32,64,1]{1,0,2,3:T(8,128)(2,1)} copy(bf16[32,32,64,1]{3,2,1,0:T(8,128)(2,1)} %get-tuple-element.42) | data formatting | bytes 262144
  44.8 3.2 collective-permute-start.2
  48.0 19.4 %copy.542 = bf16[32,32,64,1]{1,0,2,3:T(8,128)(2,1)} copy(bf16[32,32,64,1]{3,2,1,0:T(8,128)(2,1)} %get-tuple-element.41) | data formatting | bytes 262144
  67.3 1.3 collective-permute-start.3
  68.6 3.4 fusion.92
  72.7 1.3 collective-permute-start.1
  74.8 5.5 collective-permute-start
  80.3 21.9 %copy_convert_fusion = f32[32,32,64,128]{3,0,1,2:T(8,128)} fusion(bf16[32,32,64,128]{3,2,1,0:T(8,128)(2,1)} %param.10), kind=kLoop, calls=%fused_computation.3 | loop fusion | flops 8388608 | bytes 50331648 | tf_op jit(solution)/shard_map/convert_element_type | solution.py:57
  102.2 45.9 %fusion.89 = (f32[32,32,64,127]{3,0,1,2:T(8,128)}, f32[32,32,64,127]{3,0,1,2:T(8,128)}) fusion(f32[32,32,64,128]{3,0,1,2:T(8,128)} %copy_convert_fusion), kind=kLoop, calls=%fused_computation.167 | loop fusion | bytes 133169152 | tf_op jit(solution)/shard_map/slice | solution.py:44
  148.1 44.0 %fusion.88 = (f32[32,32,63,128]{3,0,1,2:T(8,128)}, f32[32,32,63,128]{3,0,1,2:T(8,128)}) fusion(f32[32,32,64,128]{3,0,1,2:T(8,128)} %copy_convert_fusion), kind=kLoop, calls=%fused_computation.166 | loop fusion | bytes 132120576 | tf_op jit(solution)/shard_map/slice | solution.py:44
  192.1 41.5 %fusion.87 = (f32[32,31,64,128]{3,0,1,2:T(8,128)}, f32[32,31,64,128]{3,0,1,2:T(8,128)}) fusion(f32[32,32,64,128]{3,0,1,2:T(8,128)} %copy_convert_fusion), kind=kLoop, calls=%fused_computation.165 | loop fusion | bytes 130023424 | tf_op jit(solution)/shard_map/slice | solution.py:44
  234.2 3.3 select_add_fusion
  238.5 34.2 %fusion.8 = f32[32,32]{1,0:T(8,128)S(1)} fusion(bf16[32,32,64,128]{3,2,1,0:T(8,128)(2,1)} %param.10), kind=kOutput, calls=%fused_computation.18 | convolution fusion | flops 536870912 | bytes 16781312 | tf_op jit(solution)/shard_map/dot_general | solution.py:67
  273.4 71.5 %multiply_convert_fusion = bf16[32,32,64,128]{3,0,1,2:T(8,128)(2,1)} fusion(f32[32,32,64,127]{3,0,1,2:T(8,128)} %get-tuple-element.40, f32[32,32,64,127]{3,0,1,2:T(8,128)} %get-tuple-element.39, f32[32,32,63,128]{3,0,1,2:T(8,128)} %get-tuple-element.38, f32[32,32,63,128]{3,0,1,2:T(8,128)} %get-tuple-element.37, f32[32,31,64,128]{3,0,1,2:T(8,128)} %get-tuple-element.36, ...), kind=kLoop, calls=%fused_computation | loop fusion | flops 83886080 | bytes 232259584 | tf_op jit(solution)/shard_map/convert_element_type | solution.py:85
  344.9 25.9 %fusion.91 = (bf16[32,32,64,1]{3,0,1,2:T(8,128)(2,1)}, bf16[32,32,64,1]{3,0,1,2:T(8,128)(2,1)}) fusion(bf16[32,32,64,128]{3,0,1,2:T(8,128)(2,1)} %multiply_convert_fusion), kind=kLoop, calls=%fused_computation.169 | loop fusion | bytes 524288 | tf_op jit(solution)/shard_map/slice | solution.py:91
  370.8 13.5 %fusion.14 = f32[32,32]{1,0:T(8,128)} fusion(f32[32,32]{1,0:T(8,128)S(1)} %fusion.8, bf16[32,32,64,128]{3,0,1,2:T(8,128)(2,1)} %multiply_convert_fusion), kind=kOutput, calls=%fused_computation.20 | convolution fusion | flops 536871936 | bytes 16785408 | tf_op jit(solution)/shard_map/dot_general | solution.py:67
  385.6 21.2 %copy.385 = bf16[32,32,64,1]{2,1,0,3:T(8,128)(2,1)S(1)} copy(bf16[32,32,64,1]{3,0,1,2:T(8,128)(2,1)} %get-tuple-element.44) | data formatting | bytes 262144 | tf_op jit(solution)/shard_map/slice | solution.py:90
  407.5 21.4 %copy.393 = bf16[32,32,64,1]{2,1,0,3:T(8,128)(2,1)S(1)} copy(bf16[32,32,64,1]{3,0,1,2:T(8,128)(2,1)} %get-tuple-element.43) | data formatting | bytes 262144 | tf_op jit(solution)/shard_map/slice | solution.py:91
  430.7 3.1 copy.408
  434.7 1.2 multiply_convert_fusion.2
  436.7 1.2 multiply_convert_fusion.1
  441.6 3.1 copy.415
  444.9 3.4 copy.416
  448.6 3.1 copy.418
  451.9 3.4 copy.419
  455.3 1.7 copy.417
  457.6 1.6 copy.499
  459.2 1.8 convolution_bitcast_fusion
  462.9 1.2 fusion.17
  464.4 3.9 copy.412
  468.5 4.2 copy.413
  473.7 1.2 fusion.18
  475.2 3.9 copy.409
  479.3 4.2 copy.410
  485.3 1.6 copy.411
  488.9 1.6 copy.414
  490.5 3.2 copy.401
  494.9 3.9 copy.421
  499.0 4.2 copy.422
  504.3 4.0 copy.423
  508.5 4.1 copy.424
  512.7 1.9 fusion.96
  516.0 3.9 copy.425
  520.1 4.1 copy.426
  524.2 1.2 copy.544
  526.6 3.9 copy.427
  530.7 4.2 copy.428
  534.9 7.7 %stack.75 = f32[21,2,8,2,4,4,2]{0,2,6,5,4,3,1:T(8,128)} concatenate(f32[1,2,8,2,4,4,2]{0,2,6,5,4,3,1:T(8,128)S(1)} %copy.408, f32[1,2,8,2,4,4,2]{0,2,6,5,4,3,1:T(8,128)} %copy.409, f32[1,2,8,2,4,4,2]{0,2,6,5,4,3,1:T(8,128)} %copy.410, f32[1,2,8,2,4,4,2]{0,2,6,5,4,3,1:T(8,128)} %copy.411, f32[1,2,8,2,4,4,2]{0,2,6,5,4,3,1:T(8,128)} %copy.412, f32[1,2,8,2,4,4,2]{0,2,6,5,4,3,1:T(8,128)} %copy.413, ...), dimensions={0} | concatenate | bytes 172032 | tf_op jit(solution)/shard_map/stack | solution.py:108
  542.5 2.9 copy.429
  546.5 5.5 all-to-all-start
  563.8 4.5 all-to-all-start.1
  568.3 4.3 all-to-all-done.1
  575.7 5.2 all_gather.18
  581.1 31.4 %all_gather.19 = f32[64,2,8,2,2]{0,4,3,1,2:T(2,128)S(1)} all-gather(f32[64,2,1,2,2]{0,4,3,1,2:T(2,128)S(1)} %copy.471), channel_id=1, replica_groups=mesh['row'=8,'col'=4] {'row'}, dimensions={2}, use_global_device_ids=true | all-gather | bytes 18432 | tf_op jit(solution)/shard_map/all_gather | solution.py:183
  612.6 5.8 cholesky.44
  619.8 4.9 custom-call.6
  625.0 30.7 %all_gather.20 = bf16[64,2,8,2,32]{0,4,3,1,2:T(8,128)(2,1)S(1)} all-gather(bf16[64,2,1,2,32]{0,4,3,1,2:T(8,128)(2,1)S(1)} %bitcast.334), channel_id=1, replica_groups=mesh['row'=8,'col'=4] {'row'}, dimensions={2}, use_global_device_ids=true | all-gather | bytes 147456 | tf_op jit(solution)/shard_map/all_gather | solution.py:192
  656.2 5.2 all_gather.21
  661.8 30.6 %all_gather.22 = f32[64,2,8,2,2]{0,4,3,1,2:T(2,128)S(1)} all-gather(f32[64,2,1,2,2]{0,4,3,1,2:T(2,128)S(1)} %copy.479), channel_id=1, replica_groups=mesh['row'=8,'col'=4] {'row'}, dimensions={2}, use_global_device_ids=true | all-gather | bytes 18432 | tf_op jit(solution)/shard_map/all_gather | solution.py:183
  692.6 5.8 cholesky.55
  699.8 4.9 custom-call.7
  705.0 30.7 %all_gather.23 = bf16[64,2,8,2,32]{0,4,3,1,2:T(8,128)(2,1)S(1)} all-gather(bf16[64,2,1,2,32]{0,4,3,1,2:T(8,128)(2,1)S(1)} %bitcast.335), channel_id=1, replica_groups=mesh['row'=8,'col'=4] {'row'}, dimensions={2}, use_global_device_ids=true | all-gather | bytes 147456 | tf_op jit(solution)/shard_map/all_gather | solution.py:192
  736.1 1.2 reshape.1011
  (177 shorter events, 48.0 us)
Async XLA Ops:
  44.8 389.9 %collective-permute-start.2 = (bf16[32,32,1,64]{1,0,3,2:T(8,128)(2,1)}, bf16[32,32,1,64]{1,0,3,2:T(8,128)(2,1)}, u32[]{:S(2)}, u32[]{:S(2)}) collective-permute-start(bf16[32,32,1,64]{1,0,3,2:T(8,128)(2,1)} %bitcast.32), channel_id=1, source_target_pairs={{0,1},{1,2},{2,3},{4,5},{5,6},{6,7},{8,9},{9,10},{10,11},{12,13},{... | collective-permute-start | bytes 393224 | tf_op jit(solution)/shard_map/ppermute | solution.py:19
  67.3 369.4 %collective-permute-start.3 = (bf16[32,32,1,64]{1,0,3,2:T(8,128)(2,1)}, bf16[32,32,1,64]{1,0,3,2:T(8,128)(2,1)}, u32[]{:S(2)}, u32[]{:S(2)}) collective-permute-start(bf16[32,32,1,64]{1,0,3,2:T(8,128)(2,1)} %bitcast.43), channel_id=1, source_target_pairs={{1,0},{2,1},{3,2},{5,4},{6,5},{7,6},{9,8},{10,9},{11,10},{13,12},{... | collective-permute-start | bytes 393224 | tf_op jit(solution)/shard_map/ppermute | solution.py:21
  72.7 389.1 %collective-permute-start.1 = (bf16[32,32,1,128]{3,1,0,2:T(8,128)(2,1)}, bf16[32,32,1,128]{3,1,0,2:T(8,128)(2,1)}, u32[]{:S(2)}, u32[]{:S(2)}) collective-permute-start(bf16[32,32,1,128]{3,1,0,2:T(8,128)(2,1)} %copy.540), channel_id=1, source_target_pairs={{4,0},{8,4},{12,8},{16,12},{20,16},{24,20},{28,24},{5,1},{9,5},{13... | collective-permute-start | bytes 786440 | tf_op jit(solution)/shard_map/ppermute | solution.py:21
  74.8 397.9 %collective-permute-start = (bf16[32,32,1,128]{3,1,2,0:T(8,128)(2,1)}, bf16[32,32,1,128]{3,1,2,0:T(8,128)(2,1)}, u32[]{:S(2)}, u32[]{:S(2)}) collective-permute-start(bf16[32,32,1,128]{3,1,2,0:T(8,128)(2,1)} %copy.539), channel_id=1, source_target_pairs={{0,4},{4,8},{8,12},{12,16},{16,20},{20,24},{24,28},{1,5},{5,9},{9,... | collective-permute-start | bytes 786440 | tf_op jit(solution)/shard_map/ppermute | solution.py:19
  192.1 41.5 %copy-start.4 = (f32[4]{0:T(128)S(1)}, f32[4]{0:T(128)}, u32[]{:S(2)}) copy-start(f32[4]{0:T(128)} %param.12) | copy-start | bytes 52
  192.1 42.2 %copy-start = (s32[32,64,128]{2,1,0:T(8,128)S(1)}, s32[32,64,128]{2,1,0:T(8,128)}, u32[]{:S(2)}) copy-start(s32[32,64,128]{2,1,0:T(8,128)} %param.11) | copy-start | bytes 3145732
  440.2 85.3 %copy-start.1 = (f32[32]{0:T(128)S(1)}, f32[32]{0:T(128)}, u32[]{:S(2)}) copy-start(f32[32]{0:T(128)} %get-tuple-element.31) | copy-start | bytes 388
  441.1 183.6 %copy-start.3 = (pred[128]{0:T(512)(128)(4,1)S(1)}, pred[128]{0:T(512)(128)(4,1)}, u32[]{:S(2)}) copy-start(pred[128]{0:T(512)(128)(4,1)} %broadcast_compare_fusion.3) | copy-start | bytes 388
  448.3 207.7 %copy-start.2 = (pred[32]{0:T(512)(128)(4,1)S(1)}, pred[32]{0:T(512)(128)(4,1)}, u32[]{:S(2)}) copy-start(pred[32]{0:T(512)(128)(4,1)} %iota_compare_fusion.2) | copy-start | bytes 100
  546.5 16.6 %all-to-all-start = ((f32[8,4,672]{2,1,0:T(4,128)}), f32[8,4,672]{2,1,0:T(4,128)S(1)}, u32[]{:S(2)}, u32[]{:S(2)}) async-start(f32[8,4,672]{2,1,0:T(4,128)} %copy.430), calls=%async_computation | async-start | bytes 196608 | tf_op jit(solution)/shard_map/all_to_all | solution.py:160
  563.8 8.8 %all-to-all-start.1 = ((f32[8,4,672]{2,0,1:T(8,128)}), f32[8,4,672]{2,0,1:T(8,128)S(1)}, u32[]{:S(2)}, u32[]{:S(2)}) async-start(f32[8,4,672]{2,0,1:T(8,128)} %copy.431), calls=%async_computation.1 | async-start | bytes 196608 | tf_op jit(solution)/shard_map/all_to_all | solution.py:159
where the time goes:
time: 749 us; the launch traced here: 738 us
  local copies, waits for them, and re-layouts  388 us (52%)
  blocking collectives  134 us (18%)
  other arithmetic  130 us (17%)
  matrix products  59.1 us (8%)
  starting transfers between devices  21.3 us (3%)
    slice x3, local copies, waits for them, and re-layouts, from_next(): inner = lax.slice_in_dim(field, 1, count, axis=axis)  131 us
    another operation x35, local copies, waits for them, and re-layouts, local_tiles(): return jnp.stack(tiles)  77.4 us
    convert_element_type x1, other arithmetic, local_tiles(): flux = (laplace_own(own) * cell_root).astype(jnp.bfloat16)  71.5 us
    all_gather x2, blocking collectives, body(): diag_all = lax.all_gather(diag_part, 'row', axis=2, tiled=True)  62 us
    all_gather x2, blocking collectives, body(): lax.all_gather(solved.reshape(width, row_blocks, 1, NB, n_sub).astype(jnp...  61.5 us
    dot_general x14, matrix products, contract_cells(): lax.dot_general(flat_left, flat_right, (((1,), (1,)), ((), ())), preferre...  58.3 us
    slice x2, local copies, waits for them, and re-layouts, local_tiles(): flux[:, :, :, -1]  47.3 us
    unnamed x16, local copies, waits for them, and re-layouts  41.7 us
  transfers between devices with their start and end apart: 6, of which 1 were waited for; matrix products, arithmetic and copies ran while one was open for 58% of the time, Pallas kernels for 0%

commit v1 on v0

--- a/solution.py
+++ b/solution.py
@@ -180,7 +180,7 @@
         part = local[first:last].reshape(PSUB, col_blocks, 1, NB, rows_here)
         whole = lax.all_gather(part, "col", axis=2, tiled=True).reshape(width, rows_here)
         diag_part = whole.reshape(width, row_blocks, 1, NB, n_sub)[:, :, :, :, first:last]
-        diag_all = lax.all_gather(diag_part, "row", axis=2, tiled=True)
+        diag_all = jnp.concatenate(lax.all_gather(diag_part, axis_name="row"), axis=2)
         diag = diag_all.transpose(0, 4, 1, 2, 3).reshape(width, width).T
         low = jnp.linalg.cholesky(diag)
         solved = lax.linalg.triangular_solve(low, whole, left_side=True, lower=True)

time: 749 us -> 755 us (level)
  transfers between devices with their start and end apart: 6 -> 6, of which waited for: 1 -> 1; matrix products, arithmetic and copies ran while one was open for 58% -> 57% of each run, Pallas kernels for 0% -> 0%
where the time goes in v1:
time: 755 us; the launch traced here: 744 us
  local copies, waits for them, and re-layouts  389 us (52%)
  blocking collectives  139 us (18%)
  other arithmetic  130 us (17%)
  matrix products  59.1 us (8%)
  starting transfers between devices  21.4 us (3%)
    slice x3, local copies, waits for them, and re-layouts, from_next(): inner = lax.slice_in_dim(field, 1, count, axis=axis)  131 us
    another operation x35, local copies, waits for them, and re-layouts, local_tiles(): return jnp.stack(tiles)  77.4 us
    convert_element_type x1, other arithmetic, local_tiles(): flux = (laplace_own(own) * cell_root).astype(jnp.bfloat16)  71.5 us
    all_gather x2, blocking collectives, body(): lax.all_gather(diag_part, axis_name='row')  66.7 us
    all_gather x2, blocking collectives, body(): lax.all_gather(solved.reshape(width, row_blocks, 1, NB, n_sub).astype(jnp...  61.5 us
    dot_general x14, matrix products, contract_cells(): lax.dot_general(flat_left, flat_right, (((1,), (1,)), ((), ())), preferre...  58.2 us
    slice x2, local copies, waits for them, and re-layouts, local_tiles(): flux[:, :, :, -1]  47.3 us
    unnamed x16, local copies, waits for them, and re-layouts  41.7 us
  transfers between devices with their start and end apart: 6, of which 1 were waited for; matrix products, arithmetic and copies ran while one was open for 57% of the time, Pallas kernels for 0%

profile of v1, /device:TPU:0, one launch (start us, length us, event | category | flops | bytes accessed | tf_op | source)
XLA Modules:
  0.0 743.8 jit_solution(11160922071887930678)
XLA Ops:
  0.0 25.4 %fusion.90 = (bf16[32,32,64,1]{3,2,1,0:T(8,128)(2,1)}, bf16[32,32,64,1]{3,2,1,0:T(8,128)(2,1)}) fusion(bf16[32,32,64,128]{3,2,1,0:T(8,128)(2,1)} %param.10), kind=kLoop, calls=%fused_computation.170 | loop fusion | bytes 524288 | tf_op jit(solution)/shard_map/slice | solution.py:75
  25.4 19.4 %copy.551 = bf16[32,32,64,1]{1,0,2,3:T(8,128)(2,1)} copy(bf16[32,32,64,1]{3,2,1,0:T(8,128)(2,1)} %get-tuple-element.42) | data formatting | bytes 262144
  44.8 3.2 collective-permute-start.2
  48.0 19.4 %copy.552 = bf16[32,32,64,1]{1,0,2,3:T(8,128)(2,1)} copy(bf16[32,32,64,1]{3,2,1,0:T(8,128)(2,1)} %get-tuple-element.41) | data formatting | bytes 262144
  67.3 1.3 collective-permute-start.3
  68.6 3.4 fusion.92
  72.7 1.3 collective-permute-start.1
  74.8 5.5 collective-permute-start
  80.3 21.9 %copy_convert_fusion = f32[32,32,64,128]{3,0,1,2:T(8,128)} fusion(bf16[32,32,64,128]{3,2,1,0:T(8,128)(2,1)} %param.10), kind=kLoop, calls=%fused_computation.3 | loop fusion | flops 8388608 | bytes 50331648 | tf_op jit(solution)/shard_map/convert_element_type | solution.py:57
  102.2 45.9 %fusion.89 = (f32[32,32,64,127]{3,0,1,2:T(8,128)}, f32[32,32,64,127]{3,0,1,2:T(8,128)}) fusion(f32[32,32,64,128]{3,0,1,2:T(8,128)} %copy_convert_fusion), kind=kLoop, calls=%fused_computation.169 | loop fusion | bytes 133169152 | tf_op jit(solution)/shard_map/slice | solution.py:44
  148.1 44.0 %fusion.88 = (f32[32,32,63,128]{3,0,1,2:T(8,128)}, f32[32,32,63,128]{3,0,1,2:T(8,128)}) fusion(f32[32,32,64,128]{3,0,1,2:T(8,128)} %copy_convert_fusion), kind=kLoop, calls=%fused_computation.168 | loop fusion | bytes 132120576 | tf_op jit(solution)/shard_map/slice | solution.py:44
  192.1 41.5 %fusion.87 = (f32[32,31,64,128]{3,0,1,2:T(8,128)}, f32[32,31,64,128]{3,0,1,2:T(8,128)}) fusion(f32[32,32,64,128]{3,0,1,2:T(8,128)} %copy_convert_fusion), kind=kLoop, calls=%fused_computation.167 | loop fusion | bytes 130023424 | tf_op jit(solution)/shard_map/slice | solution.py:44
  234.2 3.3 select_add_fusion
  238.5 34.2 %fusion.8 = f32[32,32]{1,0:T(8,128)S(1)} fusion(bf16[32,32,64,128]{3,2,1,0:T(8,128)(2,1)} %param.10), kind=kOutput, calls=%fused_computation.18 | convolution fusion | flops 536870912 | bytes 16781312 | tf_op jit(solution)/shard_map/dot_general | solution.py:67
  273.4 71.5 %multiply_convert_fusion = bf16[32,32,64,128]{3,0,1,2:T(8,128)(2,1)} fusion(f32[32,32,64,127]{3,0,1,2:T(8,128)} %get-tuple-element.40, f32[32,32,64,127]{3,0,1,2:T(8,128)} %get-tuple-element.39, f32[32,32,63,128]{3,0,1,2:T(8,128)} %get-tuple-element.38, f32[32,32,63,128]{3,0,1,2:T(8,128)} %get-tuple-element.37, f32[32,31,64,128]{3,0,1,2:T(8,128)} %get-tuple-element.36, ...), kind=kLoop, calls=%fused_computation | loop fusion | flops 83886080 | bytes 232259584 | tf_op jit(solution)/shard_map/convert_element_type | solution.py:85
  344.9 25.9 %fusion.91 = (bf16[32,32,64,1]{3,0,1,2:T(8,128)(2,1)}, bf16[32,32,64,1]{3,0,1,2:T(8,128)(2,1)}) fusion(bf16[32,32,64,128]{3,0,1,2:T(8,128)(2,1)} %multiply_convert_fusion), kind=kLoop, calls=%fused_computation.171 | loop fusion | bytes 524288 | tf_op jit(solution)/shard_map/slice | solution.py:91
  370.8 13.5 %fusion.14 = f32[32,32]{1,0:T(8,128)} fusion(f32[32,32]{1,0:T(8,128)S(1)} %fusion.8, bf16[32,32,64,128]{3,0,1,2:T(8,128)(2,1)} %multiply_convert_fusion), kind=kOutput, calls=%fused_computation.20 | convolution fusion | flops 536871936 | bytes 16785408 | tf_op jit(solution)/shard_map/dot_general | solution.py:67
  385.6 21.2 %copy.391 = bf16[32,32,64,1]{2,1,0,3:T(8,128)(2,1)S(1)} copy(bf16[32,32,64,1]{3,0,1,2:T(8,128)(2,1)} %get-tuple-element.44) | data formatting | bytes 262144 | tf_op jit(solution)/shard_map/slice | solution.py:90
  407.5 21.4 %copy.399 = bf16[32,32,64,1]{2,1,0,3:T(8,128)(2,1)S(1)} copy(bf16[32,32,64,1]{3,0,1,2:T(8,128)(2,1)} %get-tuple-element.43) | data formatting | bytes 262144 | tf_op jit(solution)/shard_map/slice | solution.py:91
  430.7 3.1 copy.414
  434.7 1.2 multiply_convert_fusion.2
  436.7 1.2 multiply_convert_fusion.1
  441.6 3.1 copy.421
  444.9 3.4 copy.422
  448.6 3.1 copy.424
  451.9 3.4 copy.425
  455.3 1.6 copy.423
  457.6 1.6 copy.507
  459.2 1.8 convolution_bitcast_fusion
  462.9 1.2 fusion.17
  464.4 3.9 copy.418
  468.5 4.2 copy.419
  473.7 1.2 fusion.18
  475.2 3.9 copy.415
  479.3 4.2 copy.416
  485.3 1.6 copy.417
  488.8 1.6 copy.420
  490.5 3.2 copy.407
  494.9 3.9 copy.427
  498.9 4.2 copy.428
  504.3 4.0 copy.429
  508.5 4.1 copy.430
  512.7 1.9 fusion.96
  516.0 3.9 copy.431
  520.1 4.1 copy.432
  524.2 1.2 copy.554
  526.6 3.9 copy.433
  530.7 4.2 copy.434
  534.9 7.7 %stack.75 = f32[21,2,8,2,4,4,2]{0,2,6,5,4,3,1:T(8,128)} concatenate(f32[1,2,8,2,4,4,2]{0,2,6,5,4,3,1:T(8,128)S(1)} %copy.414, f32[1,2,8,2,4,4,2]{0,2,6,5,4,3,1:T(8,128)} %copy.415, f32[1,2,8,2,4,4,2]{0,2,6,5,4,3,1:T(8,128)} %copy.416, f32[1,2,8,2,4,4,2]{0,2,6,5,4,3,1:T(8,128)} %copy.417, f32[1,2,8,2,4,4,2]{0,2,6,5,4,3,1:T(8,128)} %copy.418, f32[1,2,8,2,4,4,2]{0,2,6,5,4,3,1:T(8,128)} %copy.419, ...), dimensions={0} | concatenate | bytes 172032 | tf_op jit(solution)/shard_map/stack | solution.py:108
  542.5 2.9 copy.435
  546.5 5.5 all-to-all-start
  563.8 4.5 all-to-all-start.1
  568.3 4.3 all-to-all-done.1
  575.7 5.2 all_gather.24
  581.0 33.8 %all-gather = f32[512,2,1,2,2]{4,3,2,1,0:T(2,128)S(1)} all-gather(f32[64,2,1,2,2]{4,3,2,1,0:T(2,128)S(1)} %slice_bitcast_fusion.5), channel_id=2, replica_groups=mesh['row'=8,'col'=4] {'row'}, dimensions={0}, use_global_device_ids=true | all-gather | bytes 18432 | tf_op jit(solution)/shard_map/all_gather | solution.py:183
  615.7 5.8 cholesky.44
  622.9 4.9 custom-call.6
  628.2 30.8 %all_gather.27 = bf16[64,2,8,2,32]{0,4,3,1,2:T(8,128)(2,1)S(1)} all-gather(bf16[64,2,1,2,32]{0,4,3,1,2:T(8,128)(2,1)S(1)} %bitcast.349), channel_id=1, replica_groups=mesh['row'=8,'col'=4] {'row'}, dimensions={2}, use_global_device_ids=true | all-gather | bytes 147456 | tf_op jit(solution)/shard_map/all_gather | solution.py:192
  659.4 5.2 all_gather.28
  664.9 32.9 %all-gather.1 = f32[512,2,1,2,2]{4,3,2,1,0:T(2,128)S(1)} all-gather(f32[64,2,1,2,2]{4,3,2,1,0:T(2,128)S(1)} %slice_bitcast_fusion.4), channel_id=3, replica_groups=mesh['row'=8,'col'=4] {'row'}, dimensions={0}, use_global_device_ids=true | all-gather | bytes 18432 | tf_op jit(solution)/shard_map/all_gather | solution.py:183
  698.8 5.8 cholesky.55
  706.0 4.9 custom-call.7
  711.2 30.7 %all_gather.31 = bf16[64,2,8,2,32]{0,4,3,1,2:T(8,128)(2,1)S(1)} all-gather(bf16[64,2,1,2,32]{0,4,3,1,2:T(8,128)(2,1)S(1)} %bitcast.351), channel_id=1, replica_groups=mesh['row'=8,'col'=4] {'row'}, dimensions={2}, use_global_device_ids=true | all-gather | bytes 147456 | tf_op jit(solution)/shard_map/all_gather | solution.py:192
  742.3 1.2 reshape.1027
  (178 shorter events, 49.5 us)
Async XLA Ops:
  44.8 389.9 %collective-permute-start.2 = (bf16[32,32,1,64]{1,0,3,2:T(8,128)(2,1)}, bf16[32,32,1,64]{1,0,3,2:T(8,128)(2,1)}, u32[]{:S(2)}, u32[]{:S(2)}) collective-permute-start(bf16[32,32,1,64]{1,0,3,2:T(8,128)(2,1)} %bitcast.32), channel_id=1, source_target_pairs={{0,1},{1,2},{2,3},{4,5},{5,6},{6,7},{8,9},{9,10},{10,11},{12,13},{... | collective-permute-start | bytes 393224 | tf_op jit(solution)/shard_map/ppermute | solution.py:19
  67.3 369.4 %collective-permute-start.3 = (bf16[32,32,1,64]{1,0,3,2:T(8,128)(2,1)}, bf16[32,32,1,64]{1,0,3,2:T(8,128)(2,1)}, u32[]{:S(2)}, u32[]{:S(2)}) collective-permute-start(bf16[32,32,1,64]{1,0,3,2:T(8,128)(2,1)} %bitcast.43), channel_id=1, source_target_pairs={{1,0},{2,1},{3,2},{5,4},{6,5},{7,6},{9,8},{10,9},{11,10},{13,12},{... | collective-permute-start | bytes 393224 | tf_op jit(solution)/shard_map/ppermute | solution.py:21
  72.7 389.1 %collective-permute-start.1 = (bf16[32,32,1,128]{3,1,0,2:T(8,128)(2,1)}, bf16[32,32,1,128]{3,1,0,2:T(8,128)(2,1)}, u32[]{:S(2)}, u32[]{:S(2)}) collective-permute-start(bf16[32,32,1,128]{3,1,0,2:T(8,128)(2,1)} %copy.550), channel_id=1, source_target_pairs={{4,0},{8,4},{12,8},{16,12},{20,16},{24,20},{28,24},{5,1},{9,5},{13... | collective-permute-start | bytes 786440 | tf_op jit(solution)/shard_map/ppermute | solution.py:21
  74.8 397.9 %collective-permute-start = (bf16[32,32,1,128]{3,1,2,0:T(8,128)(2,1)}, bf16[32,32,1,128]{3,1,2,0:T(8,128)(2,1)}, u32[]{:S(2)}, u32[]{:S(2)}) collective-permute-start(bf16[32,32,1,128]{3,1,2,0:T(8,128)(2,1)} %copy.549), channel_id=1, source_target_pairs={{0,4},{4,8},{8,12},{12,16},{16,20},{20,24},{24,28},{1,5},{5,9},{9,... | collective-permute-start | bytes 786440 | tf_op jit(solution)/shard_map/ppermute | solution.py:19
  192.1 41.5 %copy-start.4 = (f32[4]{0:T(128)S(1)}, f32[4]{0:T(128)}, u32[]{:S(2)}) copy-start(f32[4]{0:T(128)} %param.12) | copy-start | bytes 52
  192.1 42.2 %copy-start = (s32[32,64,128]{2,1,0:T(8,128)S(1)}, s32[32,64,128]{2,1,0:T(8,128)}, u32[]{:S(2)}) copy-start(s32[32,64,128]{2,1,0:T(8,128)} %param.11) | copy-start | bytes 3145732
  440.2 85.3 %copy-start.1 = (f32[32]{0:T(128)S(1)}, f32[32]{0:T(128)}, u32[]{:S(2)}) copy-start(f32[32]{0:T(128)} %get-tuple-element.31) | copy-start | bytes 388
  444.9 182.9 %copy-start.3 = (pred[128]{0:T(512)(128)(4,1)S(1)}, pred[128]{0:T(512)(128)(4,1)}, u32[]{:S(2)}) copy-start(pred[128]{0:T(512)(128)(4,1)} %broadcast_compare_fusion.3) | copy-start | bytes 388
  455.3 203.9 %copy-start.2 = (pred[32]{0:T(512)(128)(4,1)S(1)}, pred[32]{0:T(512)(128)(4,1)}, u32[]{:S(2)}) copy-start(pred[32]{0:T(512)(128)(4,1)} %iota_compare_fusion.2) | copy-start | bytes 100
  546.5 16.6 %all-to-all-start = ((f32[8,4,672]{2,1,0:T(4,128)}), f32[8,4,672]{2,1,0:T(4,128)S(1)}, u32[]{:S(2)}, u32[]{:S(2)}) async-start(f32[8,4,672]{2,1,0:T(4,128)} %copy.436), calls=%async_computation | async-start | bytes 196608 | tf_op jit(solution)/shard_map/all_to_all | solution.py:160
  563.8 8.8 %all-to-all-start.1 = ((f32[8,4,672]{2,0,1:T(8,128)}), f32[8,4,672]{2,0,1:T(8,128)S(1)}, u32[]{:S(2)}, u32[]{:S(2)}) async-start(f32[8,4,672]{2,0,1:T(8,128)} %copy.437), calls=%async_computation.1 | async-start | bytes 196608 | tf_op jit(solution)/shard_map/all_to_all | solution.py:159
